TPU v7x, 256 devices: a whole 4x4x8 slice. The times are simulated.
256 devices in a mesh: grp: 8 (over z_lo, core), dev: 32 (over z_hi, x, y).
Axes of the slice: x: 4, y: 4, z: 8 (z_hi: 2, z_lo: 4; z = z_hi * 4 + z_lo), core: 2. Of those that a mesh axis runs over, the one named last changes fastest.
Arguments:
- images: bfloat16 [131072, 64, 128], P(('grp', 'dev')), may hold values from -16 to 16
- test_maps: bfloat16 [64, 128, 32], replicated, may hold values from -6 to 6
- counts: int32 [64], replicated, may hold values from 24 to 64, as said below
Outputs:
- projected: bfloat16 [131072, 64, 32], P(('grp', 'dev'))
Inputs may be any that keep to these rules, and one draw needn't show every extreme that they name: `counts`: block 0 has 64 radial functions and block 63 has 24.
All inputs are finite; a program needn't handle non-finite values.
Results may differ from a plain program's by a relative error of at most 0.0049.
Values may be sent and summed in bfloat16 or wider, within the bound.
No kernel may reach another device: no remote copies, remote signals or barrier semaphores. Data moves between devices by JAX's collectives and lax.ppermute only.
A program may use at most 64 MiB of HBM per device.

v0:
```python
import jax
import jax.numpy as jnp
from jax import lax
from jax.sharding import PartitionSpec as P


def orthonormal(summed):
    gram_matrix = jnp.einsum("krs,krt->kst", summed, summed, precision=lax.Precision.HIGHEST)
    factor = jnp.linalg.cholesky(gram_matrix)
    solved = lax.linalg.triangular_solve(
        factor, summed, left_side=False, lower=True, transpose_a=True
    )
    return solved.astype(jnp.bfloat16)


def body(images, test_maps, counts):
    columns = images.shape[2]
    radial = columns // 2
    position = lax.broadcasted_iota(jnp.int32, (images.shape[1], columns), 1) % radial
    valid_mask = (position < counts[:, None]).astype(jnp.bfloat16)
    masked = images * valid_mask[None]
    sketch = jnp.einsum(
        "ikr,krs->iks", masked, test_maps, preferred_element_type=jnp.float32
    ).astype(jnp.bfloat16)
    partial_sum = jnp.einsum("ikr,iks->krs", masked, sketch, preferred_element_type=jnp.float32)
    totals = lax.psum(partial_sum, "grp")
    owned = lax.psum_scatter(totals, "dev", scatter_dimension=0, tiled=True)
    basis_all = lax.all_gather(orthonormal(owned), "dev", axis=0, tiled=True)
    projected = jnp.einsum("ikr,krs->iks", masked, basis_all, preferred_element_type=jnp.float32)
    return projected.astype(jnp.bfloat16)


def solution(mesh):
    in_specs = (P(("grp", "dev"), None, None), P(), P())
    out_specs = P(("grp", "dev"), None, None)
    return jax.shard_map(body, mesh=mesh, in_specs=in_specs, out_specs=out_specs, check_vma=False)
```

profile of v0, /device:TPU:8, one launch (start us, length us, event | category | flops | bytes accessed | tf_op | source)
XLA Modules:
  0.0 447.4 jit_solution(9453604602450856554)
XLA Ops:
  6.5 0.0 copy-start
  6.5 0.0 reduce-scatter.2.cloned.1.call-start
  6.5 0.8 fusion.16
  7.3 7.2 %broadcast_multiply_fusion = bf16[512,64,128]{2,1,0:T(8,128)(2,1)} fusion(bf16[512,64,128]{2,1,0:T(8,128)(2,1)} %param.3, bf16[64,128]{1,0:T(8,128)(2,1)S(1)} %fusion.16), kind=kLoop, calls=%fused_computation.6 | loop fusion | flops 4194304 | bytes 16793600 | tf_op jit(solution)/shard_map/mul | solution.py:21
  14.5 0.0 copy-done
  14.5 24.3 %fusion.4 = f32[64,128,32]{1,2,0:T(8,128)} fusion(bf16[512,64,128]{2,1,0:T(8,128)(2,1)} %broadcast_multiply_fusion, bf16[64,128,32]{1,2,0:T(8,128)(2,1)S(1)} %copy-done), kind=kOutput, calls=%fused_computation.4 | convolution fusion | flops 537919488 | bytes 9961472 | tf_op jit(solution)/shard_map/ikr,iks->krs/dot_general | solution.py:25
  38.8 0.0 reduce-scatter.2.cloned.1.call-update
  38.9 222.5 %reduce-scatter.2.cloned.1.call-done = f32[2,128,32]{1,2,0:T(8,128)} async-done(((f32[64,128,32]{1,2,0:T(8,128)}), f32[2,128,32]{1,2,0:T(8,128)}) %reduce-scatter.2.cloned.1.call-update) | async-done | bytes 32784 | tf_op jit(solution)/shard_map/reduce_scatter | solution.py:27
  261.4 26.5 %psum.8 = f32[2,128,32]{1,2,0:T(8,128)S(1)} all-reduce(f32[2,128,32]{1,2,0:T(8,128)} %reduce-scatter.2.cloned.1.call-done), channel_id=1, replica_groups=mesh['grp'=8,'dev'=32] {'grp'}, use_global_device_ids=true, to_apply=%region_0.1 | all-reduce | flops 8192 | bytes 65536 | tf_op jit(solution)/shard_map/psum | solution.py:26
  287.9 0.2 fusion.17
  288.1 0.1 copy.12
  288.2 5.9 %custom-call.7 = f32[2,32,32]{2,1,0:T(8,128)S(1)} custom-call(f32[2,32,32]{2,1,0:T(8,128)S(1)} %fusion.15), custom_call_target="Cholesky" | custom-call | tf_op jit(solution)/shard_map/jit(cholesky)/cholesky | solution.py:9
  294.1 0.1 compare_reduce_fusion
  294.2 0.1 select_bitcast_fusion
  294.3 4.9 %custom-call.8 = f32[2,1,32,32]{2,3,1,0:T(8,128)S(1)} custom-call(f32[2,1,32,32]{3,2,1,0:T(8,128)S(1)} %select_bitcast_fusion), custom_call_target="InvertDiagBlocksLowerTriangular" | custom-call | tf_op jit(solution)/shard_map/triangular_solve | solution.py:10
  299.2 0.3 convolution_convert_fusion
  299.4 119.3 %all_gather.3 = bf16[64,128,32]{1,2,0:T(8,128)(2,1)S(1)} all-gather(bf16[2,128,32]{1,2,0:T(8,128)(2,1)S(1)} %convolution_convert_fusion), channel_id=1, replica_groups=mesh['grp'=8,'dev'=32] {'dev'}, dimensions={0}, use_global_device_ids=true | all-gather | bytes 540672 | tf_op jit(solution)/shard_map/all_gather | solution.py:28
  418.8 21.8 %convert_bitcast_fusion = bf16[512,64,32]{0,2,1:T(8,128)(2,1)} fusion(bf16[64,128,32]{1,2,0:T(8,128)(2,1)S(1)} %all_gather.3, bf16[512,64,128]{2,1,0:T(8,128)(2,1)} %broadcast_multiply_fusion), kind=kOutput, calls=%fused_computation.8 | convolution fusion | flops 269484032 | bytes 11010048 | tf_op jit(solution)/shard_map/ikr,krs->iks/dot_general | solution.py:29
  (6 shorter events, 0.1 us)
Async XLA Ops:
  6.5 8.0 %copy-start = (bf16[64,128,32]{1,2,0:T(8,128)(2,1)S(1)}, bf16[64,128,32]{1,2,0:T(8,128)(2,1)}, u32[]{:S(2)}) copy-start(bf16[64,128,32]{1,2,0:T(8,128)(2,1)} %param.4) | copy-start | bytes 1572868
  6.5 254.9 %reduce-scatter.2.cloned.1.call-start = ((), (), s32[]{:S(2)}) async-start(), calls=%async_computation.1 | async-start | bytes 1081344 | tf_op jit(solution)/shard_map/reduce_scatter | solution.py:27
Sparse Core Ops, SparseCore 0:
  39.0 222.4 reduce-scatter.1
where the time goes:
time: 448 us; the launch traced here: 447 us
  waiting for transfers between devices  223 us (50%)
  blocking collectives  146 us (33%)
  matrix products  46.5 us (10%)
  other arithmetic  19 us (4%)
  between operations  13.4 us (3%)
    reduce_scatter x1, waiting for transfers between devices, body(): owned = lax.psum_scatter(totals, 'dev', scatter_dimension=0, tiled=True)  223 us
    all_gather x1, blocking collectives, body(): basis_all = lax.all_gather(orthonormal(owned), 'dev', axis=0, tiled=True)  119 us
    psum x1, blocking collectives, body(): totals = lax.psum(partial_sum, 'grp')  26.5 us
    dot_general x1, matrix products, body(): jnp.einsum('ikr,iks->krs', masked, sketch, preferred_element_type=jnp.flo...  24.3 us
    dot_general x1, matrix products, body(): jnp.einsum('ikr,krs->iks', masked, basis_all, preferred_element_type=jnp....  21.8 us
  transfers between devices with their start and end apart: 1, of which 1 were waited for; matrix products, arithmetic and copies ran while one was open for 0% of the time, Pallas kernels for 0%

commit v1 on v0

--- a/solution.py
+++ b/solution.py
@@ -25,7 +25,11 @@
     partial_sum = jnp.einsum("ikr,iks->krs", masked, sketch, preferred_element_type=jnp.float32)
     totals = lax.psum(partial_sum, "grp")
     owned = lax.psum_scatter(totals, "dev", scatter_dimension=0, tiled=True)
-    basis_all = lax.all_gather(orthonormal(owned), "dev", axis=0, tiled=True)
+    block = orthonormal(owned)
+    count = lax.axis_size("dev")
+    tiles = jnp.stack([block for _ in range(count)])
+    tiles = lax.all_to_all(tiles, "dev", split_axis=0, concat_axis=0)
+    basis_all = jnp.concatenate(tiles, axis=0)
     projected = jnp.einsum("ikr,krs->iks", masked, basis_all, preferred_element_type=jnp.float32)
     return projected.astype(jnp.bfloat16)
 

time: 448 us -> 355 us (0.79)
  blocking collectives: 146 us -> 53 us
    all_gather x1 -> x0, blocking collectives: 119 us -> none  [body(): basis_all = lax.all_gather(orthonormal(owned), 'dev', axis=0, tiled=True)]
    all_to_all x0 -> x1, blocking collectives: none -> 26.5 us  [body(): tiles = lax.all_to_all(tiles, 'dev', split_axis=0, concat_axis=0)]
where the time goes in v1:
time: 355 us
  waiting for transfers between devices  223 us (63%)
  blocking collectives  53 us (15%)
  matrix products  46.5 us (13%)
  other arithmetic  19 us (5%)
  between operations  13.4 us (4%)
    reduce_scatter x1, waiting for transfers between devices, body(): owned = lax.psum_scatter(totals, 'dev', scatter_dimension=0, tiled=True)  223 us
    all_to_all x1, blocking collectives, body(): tiles = lax.all_to_all(tiles, 'dev', split_axis=0, concat_axis=0)  26.5 us
    psum x1, blocking collectives, body(): totals = lax.psum(partial_sum, 'grp')  26.5 us
    dot_general x1, matrix products, body(): jnp.einsum('ikr,iks->krs', masked, sketch, preferred_element_type=jnp.flo...  24.3 us
    dot_general x1, matrix products, body(): jnp.einsum('ikr,krs->iks', masked, basis_all, preferred_element_type=jnp....  21.8 us
    mul x1, other arithmetic, body(): masked = images * valid_mask[None]  7.16 us
  transfers between devices with their start and end apart: 1, of which 1 were waited for; matrix products, arithmetic and copies ran while one was open for 0% of the time, Pallas kernels for 0%

profile of v1, /device:TPU:8, one launch (start us, length us, event | category | flops | bytes accessed | tf_op | source)
XLA Modules:
  0.0 354.7 jit_solution(4509491801229491688)
XLA Ops:
  6.5 0.0 copy-start
  6.5 0.0 reduce-scatter.2.cloned.1.call-start
  6.5 0.8 fusion.16
  7.3 7.2 %broadcast_multiply_fusion = bf16[512,64,128]{2,1,0:T(8,128)(2,1)} fusion(bf16[512,64,128]{2,1,0:T(8,128)(2,1)} %param.3, bf16[64,128]{1,0:T(8,128)(2,1)S(1)} %fusion.16), kind=kLoop, calls=%fused_computation.6 | loop fusion | flops 4194304 | bytes 16793600 | tf_op jit(solution)/shard_map/mul | solution.py:21
  14.5 0.0 copy-done
  14.5 24.3 %fusion.4 = f32[64,128,32]{1,2,0:T(8,128)} fusion(bf16[512,64,128]{2,1,0:T(8,128)(2,1)} %broadcast_multiply_fusion, bf16[64,128,32]{1,2,0:T(8,128)(2,1)S(1)} %copy-done), kind=kOutput, calls=%fused_computation.4 | convolution fusion | flops 537919488 | bytes 9961472 | tf_op jit(solution)/shard_map/ikr,iks->krs/dot_general | solution.py:25
  38.8 0.0 reduce-scatter.2.cloned.1.call-update
  38.9 222.5 %reduce-scatter.2.cloned.1.call-done = f32[2,128,32]{1,2,0:T(8,128)} async-done(((f32[64,128,32]{1,2,0:T(8,128)}), f32[2,128,32]{1,2,0:T(8,128)}) %reduce-scatter.2.cloned.1.call-update) | async-done | bytes 32784 | tf_op jit(solution)/shard_map/reduce_scatter | solution.py:27
  261.4 26.5 %psum.8 = f32[2,128,32]{1,2,0:T(8,128)S(1)} all-reduce(f32[2,128,32]{1,2,0:T(8,128)} %reduce-scatter.2.cloned.1.call-done), channel_id=1, replica_groups=mesh['grp'=8,'dev'=32] {'grp'}, use_global_device_ids=true, to_apply=%region_0.1 | all-reduce | flops 8192 | bytes 65536 | tf_op jit(solution)/shard_map/psum | solution.py:26
  287.9 0.2 fusion.17
  288.1 0.1 copy.9
  288.2 5.9 %custom-call.7 = f32[2,32,32]{2,1,0:T(8,128)S(1)} custom-call(f32[2,32,32]{2,1,0:T(8,128)S(1)} %fusion.15), custom_call_target="Cholesky" | custom-call | tf_op jit(solution)/shard_map/jit(cholesky)/cholesky | solution.py:9
  294.1 0.1 compare_reduce_fusion
  294.2 0.1 select_bitcast_fusion
  294.3 4.9 %custom-call.8 = f32[2,1,32,32]{2,3,1,0:T(8,128)S(1)} custom-call(f32[2,1,32,32]{3,2,1,0:T(8,128)S(1)} %select_bitcast_fusion), custom_call_target="InvertDiagBlocksLowerTriangular" | custom-call | tf_op jit(solution)/shard_map/triangular_solve | solution.py:10
  299.2 0.3 convolution_convert_fusion
  299.4 0.1 stack.2
  299.6 26.5 %all_to_all.5 = bf16[32,2,128,32]{2,3,1,0:T(8,128)(2,1)S(1)} all-to-all(bf16[32,2,128,32]{2,3,1,0:T(8,128)(2,1)S(1)} %stack.2), channel_id=1, replica_groups=mesh['grp'=8,'dev'=32] {'dev'}, dimensions={0} | all-to-all | bytes 1048576 | tf_op jit(solution)/shard_map/all_to_all | solution.py:31
  326.1 21.8 %convert_bitcast_fusion = bf16[512,64,32]{0,2,1:T(8,128)(2,1)} fusion(bf16[64,128,32]{1,2,0:T(8,128)(2,1)S(1)} %bitcast.20, bf16[512,64,128]{2,1,0:T(8,128)(2,1)} %broadcast_multiply_fusion), kind=kOutput, calls=%fused_computation.8 | convolution fusion | flops 269484032 | bytes 11010048 | tf_op jit(solution)/shard_map/ikr,krs->iks/dot_general | solution.py:33
  (6 shorter events, 0.1 us)
Async XLA Ops:
  6.5 8.0 %copy-start = (bf16[64,128,32]{1,2,0:T(8,128)(2,1)S(1)}, bf16[64,128,32]{1,2,0:T(8,128)(2,1)}, u32[]{:S(2)}) copy-start(bf16[64,128,32]{1,2,0:T(8,128)(2,1)} %param.4) | copy-start | bytes 1572868
  6.5 254.9 %reduce-scatter.2.cloned.1.call-start = ((), (), s32[]{:S(2)}) async-start(), calls=%async_computation.2 | async-start | bytes 1081344 | tf_op jit(solution)/shard_map/reduce_scatter | solution.py:27
Sparse Core Ops, SparseCore 0:
  39.0 222.4 reduce-scatter.1
